TPU v7x, 128 devices: a whole 4x4x4 slice. The times are simulated.
128 devices in a mesh: section: 4 (over x), dp: 8 (over z_lo, y), tensor: 4 (over z_hi, core).
Axes of the slice: x: 4, y: 4, z: 4 (z_hi: 2, z_lo: 2; z = z_hi * 2 + z_lo), core: 2. Of those that a mesh axis runs over, the one named last changes fastest.
Arguments:
- saved: bfloat16 [4, 4096, 5120], P('section', ('dp', 'tensor')), may hold values from -0.09375 to 0.09375
- weight: bfloat16 [4, 5120, 5120], P('section', None, 'tensor'), may hold values from -0.078125 to 0.078125
- out_grad: bfloat16 [4096, 5120], P(('dp', 'tensor')), may hold values from -6 to 6
Outputs:
- input_grads: bfloat16 [4, 4096, 5120], P('section', ('dp', 'tensor'))
- weight_grads: float32 [4, 5120, 5120], P('section', 'dp', 'tensor')
All inputs are finite; a program needn't handle non-finite values.
Results may differ from a plain program's by a relative error of at most 0.02.
Values may be sent and summed in bfloat16 or wider, within the bound.
A program may use at most 192 MiB of HBM per device.

v0:
```python
import jax
import jax.numpy as jnp
from jax import lax
from jax.sharding import PartitionSpec as P


def from_behind(block, axis, distance):
    devices = range(lax.axis_size(axis))
    route = [(i - distance, i) for i in devices if i - distance in devices]
    return lax.ppermute(block, axis, route)


def on_device(saved, weight, out_grad):
    activations = saved[0]
    weight_cols = weight[0]
    sections = lax.axis_size("section")
    section_index = lax.axis_index("section")
    gradient = out_grad
    own_input = jnp.zeros(out_grad.shape, jnp.bfloat16)
    kept_columns = jnp.zeros(
        (out_grad.shape[0] * lax.axis_size("tensor"), weight_cols.shape[1]), jnp.bfloat16
    )
    for rounds in range(sections):
        active = sections - 1 - rounds
        on_duty = section_index == active
        columns = lax.all_to_all(gradient, "tensor", split_axis=1, concat_axis=0, tiled=True)

        def compute(operand):
            return lax.dot_general(
                operand, weight_cols, (((1,), (1,)), ((), ())), preferred_element_type=jnp.float32
            )

        def nothing(operand):
            return jnp.zeros((operand.shape[0], weight_cols.shape[0]), jnp.float32)

        returned = lax.psum_scatter(
            lax.cond(on_duty, compute, nothing, columns).astype(jnp.bfloat16),
            "tensor",
            scatter_dimension=0,
            tiled=True,
        ).astype(jnp.float32)
        updated = (gradient.astype(jnp.float32) + returned).astype(jnp.bfloat16)
        own_input = jnp.where(on_duty, updated, own_input)
        kept_columns = jnp.where(on_duty, columns, kept_columns)
        if rounds + 1 < sections:
            gradient = from_behind(updated, "section", -1)
    gathered = lax.all_gather(activations, "tensor", axis=0, tiled=True)
    weight_grad = lax.psum_scatter(
        lax.dot_general(
            gathered, kept_columns, (((0,), (0,)), ((), ())), preferred_element_type=jnp.float32
        ).astype(jnp.bfloat16),
        "dp",
        scatter_dimension=0,
        tiled=True,
    ).astype(jnp.float32)
    return (own_input[None], weight_grad[None])


def solution(mesh):
    placed = (
        P("section", ("dp", "tensor"), None),
        P("section", None, "tensor"),
        P(("dp", "tensor"), None),
    )
    return jax.shard_map(
        on_device,
        mesh=mesh,
        in_specs=placed,
        out_specs=(P("section", ("dp", "tensor"), None), P("section", "dp", "tensor")),
        check_vma=False,
    )
```

profile of v0, /device:TPU:40, one launch (start us, length us, event | category | flops | bytes accessed | tf_op | source)
XLA Modules:
  0.0 706.9 jit_solution(3716013409856002741)
XLA Ops:
  7.2 2.5 copy.46
  9.6 4.2 all-to-all-start
  13.9 18.8 %all-to-all-done = bf16[128,4,1280]{2,0,1:T(8,128)(2,1)S(1)} async-done(((bf16[128,4,1280]{2,0,1:T(8,128)(2,1)}), bf16[128,4,1280]{2,0,1:T(8,128)(2,1)S(1)}, u32[]{:S(2)}, u32[]{:S(2)}) %all-to-all-start) | async-done | bytes 1310752 | tf_op jit(solution)/shard_map/all_to_all | solution.py:26
  33.7 3.0 conditional.4
  33.7 3.0 broadcast.8
  36.7 7.9 %copy.25 = bf16[512,5120]{0,1:T(8,128)(2,1)} copy(bf16[512,5120]{1,0:T(8,128)(2,1)} %get-tuple-element.46) | data formatting | bytes 10485760 | tf_op jit(solution)/shard_map/cond | solution.py:37
  44.7 7.9 %copy.34 = bf16[512,5120]{1,0:T(8,128)(2,1)} copy(bf16[512,5120]{0,1:T(8,128)(2,1)} %copy.25) | data formatting | bytes 10485760
  54.6 65.6 %reduce-scatter.16.cloned.1.call-done = bf16[128,5120]{1,0:T(8,128)(2,1)} async-done(((bf16[512,5120]{1,0:T(8,128)(2,1)}), bf16[128,5120]{1,0:T(8,128)(2,1)}) %reduce-scatter.16.cloned.1.call-update) | async-done | bytes 1310736
  120.3 1.8 copy.35
  122.4 1.3 collective-permute-start
  123.7 31.1 %collective-permute-done = bf16[128,5120]{0,1:T(8,128)(2,1)S(1)} collective-permute-done((bf16[128,5120]{0,1:T(8,128)(2,1)S(1)}, bf16[128,5120]{0,1:T(8,128)(2,1)S(1)}, u32[]{:S(2)}, u32[]{:S(2)}) %collective-permute-start) | collective-permute-done | bytes 1310752 | tf_op jit(solution)/shard_map/ppermute | solution.py:10
  154.8 1.4 copy.26
  156.2 3.5 all-to-all-start.1
  159.8 18.7 %all-to-all-done.1 = bf16[128,4,1280]{2,0,1:T(8,128)(2,1)S(1)} async-done(((bf16[128,4,1280]{2,0,1:T(8,128)(2,1)}), bf16[128,4,1280]{2,0,1:T(8,128)(2,1)S(1)}, u32[]{:S(2)}, u32[]{:S(2)}) %all-to-all-start.1) | async-done | bytes 1310752 | tf_op jit(solution)/shard_map/all_to_all | solution.py:26
  179.6 3.0 conditional.5
  179.6 3.0 broadcast.9
  182.6 7.9 %copy.27 = bf16[512,5120]{0,1:T(8,128)(2,1)} copy(bf16[512,5120]{1,0:T(8,128)(2,1)} %get-tuple-element.47) | data formatting | bytes 10485760 | tf_op jit(solution)/shard_map/cond | solution.py:37
  190.5 7.9 %copy.36 = bf16[512,5120]{1,0:T(8,128)(2,1)} copy(bf16[512,5120]{0,1:T(8,128)(2,1)} %copy.27) | data formatting | bytes 10485760
  198.4 67.8 %reduce-scatter.18.cloned.1.call-done = bf16[128,5120]{1,0:T(8,128)(2,1)} async-done(((bf16[512,5120]{1,0:T(8,128)(2,1)}), bf16[128,5120]{1,0:T(8,128)(2,1)}) %reduce-scatter.18.cloned.1.call-update) | async-done | bytes 1310736
  266.3 1.8 copy.37
  269.7 31.1 %collective-permute-done.1 = bf16[128,5120]{0,1:T(8,128)(2,1)S(1)} collective-permute-done((bf16[128,5120]{0,1:T(8,128)(2,1)S(1)}, bf16[128,5120]{0,1:T(8,128)(2,1)S(1)}, u32[]{:S(2)}, u32[]{:S(2)}) %collective-permute-start.1) | collective-permute-done | bytes 1310752 | tf_op jit(solution)/shard_map/ppermute | solution.py:10
  300.8 1.4 copy.28
  302.2 3.5 all-to-all-start.2
  305.8 18.7 %all-to-all-done.2 = bf16[128,4,1280]{2,0,1:T(8,128)(2,1)S(1)} async-done(((bf16[128,4,1280]{2,0,1:T(8,128)(2,1)}), bf16[128,4,1280]{2,0,1:T(8,128)(2,1)S(1)}, u32[]{:S(2)}, u32[]{:S(2)}) %all-to-all-start.2) | async-done | bytes 1310752 | tf_op jit(solution)/shard_map/all_to_all | solution.py:26
  325.6 3.0 conditional.6
  325.6 3.0 broadcast.10
  328.6 7.9 %copy.29 = bf16[512,5120]{0,1:T(8,128)(2,1)} copy(bf16[512,5120]{1,0:T(8,128)(2,1)} %get-tuple-element.48) | data formatting | bytes 10485760 | tf_op jit(solution)/shard_map/cond | solution.py:37
  336.5 7.9 %copy.38 = bf16[512,5120]{1,0:T(8,128)(2,1)} copy(bf16[512,5120]{0,1:T(8,128)(2,1)} %copy.29) | data formatting | bytes 10485760
  345.0 65.7 %reduce-scatter.20.cloned.1.call-done = bf16[128,5120]{1,0:T(8,128)(2,1)} async-done(((bf16[512,5120]{1,0:T(8,128)(2,1)}), bf16[128,5120]{1,0:T(8,128)(2,1)}) %reduce-scatter.20.cloned.1.call-update) | async-done | bytes 1310736
  410.8 1.8 copy.39
  414.2 31.1 %collective-permute-done.2 = bf16[128,5120]{0,1:T(8,128)(2,1)S(1)} collective-permute-done((bf16[128,5120]{0,1:T(8,128)(2,1)S(1)}, bf16[128,5120]{0,1:T(8,128)(2,1)S(1)}, u32[]{:S(2)}, u32[]{:S(2)}) %collective-permute-start.2) | collective-permute-done | bytes 1310752 | tf_op jit(solution)/shard_map/ppermute | solution.py:10
  445.3 1.4 copy.30
  446.7 3.5 all-to-all-start.3
  450.3 18.7 %all-to-all-done.3 = bf16[128,4,1280]{2,0,1:T(8,128)(2,1)S(1)} async-done(((bf16[128,4,1280]{2,0,1:T(8,128)(2,1)}), bf16[128,4,1280]{2,0,1:T(8,128)(2,1)S(1)}, u32[]{:S(2)}, u32[]{:S(2)}) %all-to-all-start.3) | async-done | bytes 1310752 | tf_op jit(solution)/shard_map/all_to_all | solution.py:26
  470.1 13.4 %conditional.7 = (bf16[512,5120]{1,0:T(8,128)(2,1)}) conditional(s32[]{:T(128)} %convert_element_type.83, () %tuple.38, (bf16[512,1280]{1,0:T(8,128)(2,1)S(1)}, bf16[5120,1280]{1,0:T(8,128)(2,1)}) %tuple.72), branch_computations={%region_9.10_spmd, %region_10.11_spmd} | conditional | flops 6710886400 | bytes 19660808 | solution.py:37
  470.1 13.4 %fusion.17 = bf16[512,5120]{1,0:T(8,128)(2,1)} fusion(bf16[512,1280]{1,0:T(8,128)(2,1)S(1)} %get-tuple-element.34, bf16[5120,1280]{1,0:T(8,128)(2,1)} %get-tuple-element.35), kind=kOutput, calls=%fused_computation.24 | convolution fusion | flops 6710886400 | bytes 19660800 | tf_op jit(solution)/shard_map/cond/branch_1_fun/dot_general | solution.py:29
  483.5 8.0 %copy.31 = bf16[512,5120]{0,1:T(8,128)(2,1)} copy(bf16[512,5120]{1,0:T(8,128)(2,1)} %get-tuple-element.49) | data formatting | bytes 10485760 | tf_op jit(solution)/shard_map/cond | solution.py:37
  491.4 8.0 %copy.40 = bf16[512,5120]{1,0:T(8,128)(2,1)} copy(bf16[512,5120]{0,1:T(8,128)(2,1)} %copy.31) | data formatting | bytes 10485760
  500.7 12.3 %fusion = bf16[5120,1280]{0,1:T(8,128)(2,1)} fusion(bf16[1,512,5120]{2,1,0:T(8,128)(2,1)} %all-gather.3.cloned.1.call-done, bf16[512,1280]{1,0:T(8,128)(2,1)} %bitcast.54, bf16[512,1280]{1,0:T(8,128)(2,1)} %bitcast.52, bf16[512,1280]{1,0:T(8,128)(2,1)} %bitcast.50, bf16[512,1280]{1,0:T(8,128)(2,1)S(1)} %bitcast.48, pred[]{:T(512)S(6)} %eq.13, pred[]{:T(512)S(6)} %eq.14, ...), kind=kOutput, calls=%fused_computation.1 | convolution fusion | flops 6720061440 | bytes 23592964 | tf_op jit(solution)/shard_map/dot_general | solution.py:49
  513.0 18.0 %copy.42 = bf16[5120,1280]{1,0:T(8,128)(2,1)} copy(bf16[5120,1280]{0,1:T(8,128)(2,1)} %fusion) | data formatting | bytes 26214400
  531.0 23.4 %reduce-scatter.22.cloned.1.call-done = bf16[128,5120]{1,0:T(8,128)(2,1)} async-done(((bf16[512,5120]{1,0:T(8,128)(2,1)}), bf16[128,5120]{1,0:T(8,128)(2,1)}) %reduce-scatter.22.cloned.1.call-update) | async-done | bytes 1310736
  554.4 1.8 copy.41
  556.2 1.6 fusion.3
  557.7 2.4 copy.32
  560.1 131.7 %reduce-scatter.24.cloned.1.call-done = bf16[640,1280]{1,0:T(8,128)(2,1)} async-done(((bf16[5120,1280]{1,0:T(8,128)(2,1)}), bf16[640,1280]{1,0:T(8,128)(2,1)}) %reduce-scatter.24.cloned.1.call-update) | async-done | bytes 1638416
  691.9 3.5 copy.43
  695.4 1.6 bitcast_convert_fusion
  697.0 3.0 copy.33
  (37 shorter events, 12.0 us)
Async XLA Ops:
  9.6 23.0 %all-to-all-start = ((bf16[128,4,1280]{2,0,1:T(8,128)(2,1)}), bf16[128,4,1280]{2,0,1:T(8,128)(2,1)S(1)}, u32[]{:S(2)}, u32[]{:S(2)}) async-start(bf16[128,4,1280]{2,0,1:T(8,128)(2,1)} %bitcast.42), calls=%async_computation | async-start | bytes 2621440 | tf_op jit(solution)/shard_map/all_to_all | solution.py:26
  13.9 106.4 %reduce-scatter.16.cloned.1.call-start = ((), (), s32[]{:S(2)}) async-start(), calls=%async_computation.10 | async-start | bytes 6553600
  32.6 1.1 copy-start.4
  52.5 1.3 copy-start
  122.4 32.4 %copy-start.1 = (bf16[128,5120]{0,1:T(8,128)(2,1)}, bf16[128,5120]{0,1:T(8,128)(2,1)S(1)}, u32[]{:S(2)}) copy-start(bf16[128,5120]{0,1:T(8,128)(2,1)S(1)} %add_convert_fusion.3) | copy-start | bytes 3932164
  122.4 32.4 %collective-permute-start = (bf16[128,5120]{0,1:T(8,128)(2,1)S(1)}, bf16[128,5120]{0,1:T(8,128)(2,1)S(1)}, u32[]{:S(2)}, u32[]{:S(2)}) collective-permute-start(bf16[128,5120]{0,1:T(8,128)(2,1)S(1)} %add_convert_fusion.3), channel_id=1, source_target_pairs={{32,0},{64,32},{96,64},{33,1},{65,33},{97,65},{34,2},{66,34},{98,6... | collective-permute-start | bytes 3932168 | tf_op jit(solution)/shard_map/ppermute | solution.py:10
  156.2 22.3 %all-to-all-start.1 = ((bf16[128,4,1280]{2,0,1:T(8,128)(2,1)}), bf16[128,4,1280]{2,0,1:T(8,128)(2,1)S(1)}, u32[]{:S(2)}, u32[]{:S(2)}) async-start(bf16[128,4,1280]{2,0,1:T(8,128)(2,1)} %copy.26), calls=%async_computation.1 | async-start | bytes 2621440 | tf_op jit(solution)/shard_map/all_to_all | solution.py:26
  159.8 106.5 %reduce-scatter.18.cloned.1.call-start = ((), (), s32[]{:S(2)}) async-start(), calls=%async_computation.11 | async-start | bytes 6553600
  178.5 1.1 copy-start.6
  268.4 32.4 %copy-start.2 = (bf16[128,5120]{0,1:T(8,128)(2,1)}, bf16[128,5120]{0,1:T(8,128)(2,1)S(1)}, u32[]{:S(2)}) copy-start(bf16[128,5120]{0,1:T(8,128)(2,1)S(1)} %add_convert_fusion.2) | copy-start | bytes 3932164
  268.4 32.4 %collective-permute-start.1 = (bf16[128,5120]{0,1:T(8,128)(2,1)S(1)}, bf16[128,5120]{0,1:T(8,128)(2,1)S(1)}, u32[]{:S(2)}, u32[]{:S(2)}) collective-permute-start(bf16[128,5120]{0,1:T(8,128)(2,1)S(1)} %add_convert_fusion.2), channel_id=1, source_target_pairs={{32,0},{64,32},{96,64},{33,1},{65,33},{97,65},{34,2},{66,34},{98,6... | collective-permute-start | bytes 3932168 | tf_op jit(solution)/shard_map/ppermute | solution.py:10
  302.2 22.3 %all-to-all-start.2 = ((bf16[128,4,1280]{2,0,1:T(8,128)(2,1)}), bf16[128,4,1280]{2,0,1:T(8,128)(2,1)S(1)}, u32[]{:S(2)}, u32[]{:S(2)}) async-start(bf16[128,4,1280]{2,0,1:T(8,128)(2,1)} %copy.28), calls=%async_computation.2 | async-start | bytes 2621440 | tf_op jit(solution)/shard_map/all_to_all | solution.py:26
  305.8 105.0 %reduce-scatter.20.cloned.1.call-start = ((), (), s32[]{:S(2)}) async-start(), calls=%async_computation.12 | async-start | bytes 6553600
  324.5 1.1 copy-start.7
  344.4 155.3 %all-gather.3.cloned.1.call-start = ((), (), s32[]{:S(2)}) async-start(), calls=%async_computation.9 | async-start | bytes 6553600 | tf_op jit(solution)/shard_map/all_gather | solution.py:47
  412.9 32.4 %copy-start.3 = (bf16[128,5120]{0,1:T(8,128)(2,1)}, bf16[128,5120]{0,1:T(8,128)(2,1)S(1)}, u32[]{:S(2)}) copy-start(bf16[128,5120]{0,1:T(8,128)(2,1)S(1)} %add_convert_fusion.1) | copy-start | bytes 3932164
  412.9 32.4 %collective-permute-start.2 = (bf16[128,5120]{0,1:T(8,128)(2,1)S(1)}, bf16[128,5120]{0,1:T(8,128)(2,1)S(1)}, u32[]{:S(2)}, u32[]{:S(2)}) collective-permute-start(bf16[128,5120]{0,1:T(8,128)(2,1)S(1)} %add_convert_fusion.1), channel_id=1, source_target_pairs={{32,0},{64,32},{96,64},{33,1},{65,33},{97,65},{34,2},{66,34},{98,6... | collective-permute-start | bytes 3932168 | tf_op jit(solution)/shard_map/ppermute | solution.py:10
  446.7 22.3 %all-to-all-start.3 = ((bf16[128,4,1280]{2,0,1:T(8,128)(2,1)}), bf16[128,4,1280]{2,0,1:T(8,128)(2,1)S(1)}, u32[]{:S(2)}, u32[]{:S(2)}) async-start(bf16[128,4,1280]{2,0,1:T(8,128)(2,1)} %copy.30), calls=%async_computation.3 | async-start | bytes 2621440 | tf_op jit(solution)/shard_map/all_to_all | solution.py:26
  450.3 104.1 %reduce-scatter.22.cloned.1.call-start = ((), (), s32[]{:S(2)}) async-start(), calls=%async_computation.13 | async-start | bytes 6553600
  469.0 1.1 copy-start.8
  499.4 1.3 copy-start.5
  499.4 192.4 %reduce-scatter.24.cloned.1.call-start = ((), (), s32[]{:S(2)}) async-start(), calls=%async_computation.14 | async-start | bytes 14745600
Sparse Core Ops, SparseCore 0:
  52.7 67.5 reduce-scatter.15
  198.6 67.6 reduce-scatter.17
  344.6 66.1 reduce-scatter.19
  412.4 43.7 all-gather.2
  499.6 54.8 reduce-scatter.21
  556.7 135.1 reduce-scatter.23
where the time goes:
time: 713 us; the launch traced here: 707 us
  waiting for transfers between devices  523 us (73%)
  local copies, waits for them, and re-layouts  120 us (17%)
  matrix products  25.7 us (4%)
  starting transfers between devices  19.2 us (3%)
  between operations  14.3 us (2%)
    unnamed x11, waiting for transfers between devices  355 us
    ppermute x3, waiting for transfers between devices, from_behind(): return lax.ppermute(block, axis, route)  93.3 us
    all_to_all x4, waiting for transfers between devices, on_device(): lax.all_to_all(gradient, 'tensor', split_axis=1, concat_axis=0, tiled=True)  74.8 us
    unnamed x31, local copies, waits for them, and re-layouts  72.8 us
    cond x4, local copies, waits for them, and re-layouts, on_device(): lax.cond(on_duty, compute, nothing, columns).astype(jnp.bfloat16)  31.8 us
    all_to_all x4, starting transfers between devices, on_device(): lax.all_to_all(gradient, 'tensor', split_axis=1, concat_axis=0, tiled=True)  14.9 us
  transfers between devices with their start and end apart: 13, of which 12 were waited for; matrix products, arithmetic and copies ran while one was open for 10% of the time, Pallas kernels for 0%

commit v1 on v0

v1 whole, which is shorter than its diff:
```python
import functools

import jax
import jax.numpy as jnp
from jax import lax
from jax.experimental import pallas as pl
from jax.experimental.pallas import tpu as pltpu
from jax.sharding import PartitionSpec as P

MESH = pl.DeviceIdType.MESH
BF16 = jnp.bfloat16
F32 = jnp.float32
CW = 256
NY = 4


def rdma(src, dst, send, recv, dev):
    return pltpu.make_async_remote_copy(
        src_ref=src, dst_ref=dst, send_sem=send, recv_sem=recv, device_id=dev, device_id_type=MESH
    )


def nt_dot(a, b):
    return lax.dot_general(a, b, (((1,), (1,)), ((), ())), preferred_element_type=F32)


def relay(
    og, w,
    out, gq,
    wv, g, ps, pr, own, gn,
    w_sem, w_send, w_recv, gi_send, gi_recv, x_recv, f_send, f_recv, p_send, p_recv, x_send, o_send, o_recv, loc,
):
    rows, width = og.shape
    quarter = width // 4
    half = width // 2
    nk = quarter // CW
    sections = lax.axis_size("section")
    s, d, t = lax.axis_index("section"), lax.axis_index("dp"), lax.axis_index("tensor")
    l, y = d // NY, d % NY
    h, c = t // 2, t % 2
    partner = (s, d, h * 2 + 1 - c)
    pair_t = (1 - h) * 2 + c
    pair_d = (1 - l) * NY + y
    pair = (s, pair_d, pair_t)
    pair_x = (s, pair_d, (1 - h) * 2 + 1 - c)
    up = (lax.rem(s + sections - 1, sections), d, t)
    down = (lax.rem(s + 1, sections), d, t)
    first = s == sections - 1

    barrier = pltpu.get_barrier_semaphore()
    for dev in (partner, pair, pair_x, up, down):
        pl.semaphore_signal(barrier, inc=1, device_id=dev, device_id_type=MESH)
    pl.semaphore_wait(barrier, 5)

    cols = pl.ds(pl.multiple_of(c * quarter, quarter), quarter)

    def w_rows(a, core):
        hh = (1 - h) if a == 0 else h
        return pl.ds(pl.multiple_of(hh * half + core * quarter, quarter), quarter)

    w_local = [pltpu.make_async_copy(w.at[w_rows(a, c), :], wv.at[a, :, cols], w_sem.at[a]) for a in range(2)]
    w_away = [rdma(w.at[w_rows(a, 1 - c), :], wv.at[a, :, cols], w_send.at[a], w_recv.at[a], partner) for a in range(2)]
    own_rows = pl.ds(pl.multiple_of(t * rows, rows), rows)
    pair_rows = pl.ds(pl.multiple_of(pair_t * rows, rows), rows)
    my_half = pl.ds(pl.multiple_of(h * half, half), half)
    other_half = pl.ds(pl.multiple_of((1 - h) * half, half), half)
    g_pair = rdma(og.at[:, other_half], g.at[own_rows, :], gi_send.at[0], gi_recv.at[0], pair)
    g_partner = rdma(og.at[:, my_half], g.at[own_rows, :], gi_send.at[1], gi_recv.at[1], partner)
    g_fwd = rdma(g.at[pair_rows, :], g.at[pair_rows, :], gi_send.at[2], gi_recv.at[2], partner)

    @pl.when(first)
    def _():
        g_pair.start()
        g_partner.start()

    for a in range(2):
        w_away[a].start()
        w_local[a].start()

    def x_cols(k):
        return pl.ds(pl.multiple_of(c * quarter + k * CW, CW), CW)

    def x_copy(k):
        return rdma(
            gn.at[:, pl.ds(pl.multiple_of(k * CW, CW), CW)], g.at[:, x_cols(k)], x_send.at[k], x_recv.at[k], up
        )

    def f_copy(k):
        return rdma(g.at[:, x_cols(k)], g.at[:, x_cols(k)], f_send.at[k], f_recv.at[k], partner)

    @pl.when(first)
    def _():
        here = pltpu.make_async_copy(og.at[:, my_half], g.at[own_rows, :], loc.at[0])
        here.start()
        g_pair.wait_recv()
        g_fwd.start()
        here.wait()
        g_partner.wait_recv()
        g_fwd.wait_recv()
        g_pair.wait_send()
        g_partner.wait_send()
        g_fwd.wait_send()

    @pl.when(jnp.logical_not(first))
    def _():
        def arrive(k, carry):
            x_copy(k).wait_recv()
            f_copy(k).start()
            return carry

        lax.fori_loop(0, nk, arrive, 0)

        def forwarded(k, carry):
            f_copy(k).wait_recv()
            f_copy(k).wait_send()
            return carry

        lax.fori_loop(0, nk, forwarded, 0)

    keep = pltpu.make_async_copy(g.at[:, cols], gq, loc.at[1])
    keep.start()

    for a in range(2):
        w_local[a].wait()
        w_away[a].wait_recv()
        w_away[a].wait_send()

    def p_copy(k):
        return rdma(ps.at[k], pr.at[k], p_send.at[k], p_recv.at[k], pair)

    def send_part(k, carry):
        ps[k] = nt_dot(g[...], wv[0, pl.ds(pl.multiple_of(k * CW, CW), CW), :]).astype(BF16)
        p_copy(k).start()
        return carry

    lax.fori_loop(0, nk, send_part, 0)

    def own_part(k, carry):
        own[k] = nt_dot(g[...], wv[1, pl.ds(pl.multiple_of(k * CW, CW), CW), :])
        return carry

    lax.fori_loop(0, nk, own_part, 0)

    def finish(k, carry):
        p_copy(k).wait_recv()
        total = own[k] + pr[k].astype(F32) + g[:, x_cols(k)].astype(F32)
        gn[:, pl.ds(pl.multiple_of(k * CW, CW), CW)] = total.astype(BF16)

        @pl.when(s > 0)
        def _():
            x_copy(k).start()

        return carry

    lax.fori_loop(0, nk, finish, 0)

    t_cols = pl.ds(pl.multiple_of(t * quarter, quarter), quarter)
    homes = [partner, pair, pair_x]
    blocks = [h * 2 + 1 - c, pair_t, (1 - h) * 2 + 1 - c]
    home = [
        rdma(gn.at[pl.ds(pl.multiple_of(b * rows, rows), rows), :], out.at[:, t_cols], o_send.at[i], o_recv.at[i], dev)
        for i, (dev, b) in enumerate(zip(homes, blocks))
    ]
    for copy in home:
        copy.start()
    mine = pltpu.make_async_copy(gn.at[own_rows, :], out.at[:, t_cols], loc.at[0])
    mine.start()
    mine.wait()
    keep.wait()
    for copy in home:
        copy.wait_recv()
        copy.wait_send()

    def drain(k, carry):
        p_copy(k).wait_send()

        @pl.when(s > 0)
        def _():
            x_copy(k).wait_send()

        return carry

    lax.fori_loop(0, nk, drain, 0)


def on_device(saved, weight, out_grad):
    rows, width = out_grad.shape
    quarter, half = width // 4, width // 2
    nk = quarter // CW
    dma = pltpu.SemaphoreType.DMA
    vmem = pltpu.VMEM
    own_input, columns = pl.pallas_call(
        relay,
        out_shape=(
            jax.ShapeDtypeStruct((rows, width), BF16),
            jax.ShapeDtypeStruct((4 * rows, quarter), BF16),
        ),
        in_specs=[pl.BlockSpec(memory_space=pltpu.VMEM), pl.BlockSpec(memory_space=pl.ANY)],
        out_specs=(pl.BlockSpec(memory_space=pltpu.VMEM), pl.BlockSpec(memory_space=pltpu.VMEM)),
        scratch_shapes=[
            vmem((2, quarter, half), BF16),
            vmem((4 * rows, half), BF16),
            vmem((nk, 4 * rows, CW), BF16),
            vmem((nk, 4 * rows, CW), BF16),
            vmem((nk, 4 * rows, CW), F32),
            vmem((4 * rows, quarter), BF16),
            dma((2,)), dma((2,)), dma((2,)), dma((3,)), dma((3,)),
            dma((nk,)), dma((nk,)), dma((nk,)), dma((nk,)), dma((nk,)), dma((nk,)),
            dma((3,)), dma((3,)), dma((2,)),
        ],
        compiler_params=pltpu.CompilerParams(
            collective_id=0, has_side_effects=True, vmem_limit_bytes=60 * 1024 * 1024
        ),
    )(out_grad, weight[0])

    def pick(dp_flip, h_flip, c_flip):
        route = []
        for dd in range(8):
            for tt in range(4):
                ll, yy, hh, cc = dd // NY, dd % NY, tt // 2, tt % 2
                src = dd * 4 + tt
                dst = ((ll ^ dp_flip) * NY + yy) * 4 + (hh ^ h_flip) * 2 + (cc ^ c_flip)
                route.append((src, dst))
        return route

    mine = saved[0]
    others = [
        lax.ppermute(mine, ("dp", "tensor"), pick(*flips)) for flips in ((0, 0, 1), (1, 1, 0), (1, 1, 1))
    ]
    t = lax.axis_index("tensor")
    c = t % 2
    h = t // 2
    chip = jnp.where(c == 0, jnp.concatenate([mine, others[0]]), jnp.concatenate([others[0], mine]))
    pair = jnp.where(c == 0, jnp.concatenate([others[1], others[2]]), jnp.concatenate([others[2], others[1]]))
    gathered = jnp.where(h == 0, jnp.concatenate([chip, pair]), jnp.concatenate([pair, chip]))
    weight_grad = lax.psum_scatter(
        lax.dot_general(gathered, columns, (((0,), (0,)), ((), ())), preferred_element_type=F32).astype(BF16),
        "dp",
        scatter_dimension=0,
        tiled=True,
    ).astype(F32)
    return (own_input[None], weight_grad[None])


def solution(mesh):
    placed = (
        P("section", ("dp", "tensor"), None),
        P("section", None, "tensor"),
        P(("dp", "tensor"), None),
    )
    return jax.shard_map(
        on_device,
        mesh=mesh,
        in_specs=placed,
        out_specs=(P("section", ("dp", "tensor"), None), P("section", "dp", "tensor")),
        check_vma=False,
    )
```

time: 713 us -> 420 us (0.59)
  waiting for transfers between devices: 523 us -> 137 us
  Pallas kernels: 0 us -> 244 us
  local copies, waits for them, and re-layouts: 120 us -> 1.32 us
  starting transfers between devices: 19.2 us -> 2.18 us
  matrix products: 25.7 us -> 10.2 us
    unnamed x11 -> x1, waiting for transfers between devices: 355 us -> 0.02 us
    pallas_call x0 -> x1, Pallas kernels: none -> 244 us  [on_device(): pl.pallas_call(relay, out_shape=(jax.ShapeDtypeStruct((rows, width), BF16...]
    reduce_scatter x0 -> x1, waiting for transfers between devices: none -> 137 us  [on_device(): lax.psum_scatter(lax.dot_general(gathered, columns, (((0,), (0,)), ((), (...]
    ppermute x3, waiting for transfers between devices: 93.3 us -> 0.01 us  [on_device(): lax.ppermute(mine, ('dp', 'tensor'), pick(*flips))]
    all_to_all x4 -> x0, waiting for transfers between devices: 74.8 us -> none  [on_device(): lax.all_to_all(gradient, 'tensor', split_axis=1, concat_axis=0, tiled=True)]
    unnamed x31 -> x7, local copies, waits for them, and re-layouts: 72.8 us -> 1.32 us
    cond x4 -> x0, local copies, waits for them, and re-layouts: 31.8 us -> none  [on_device(): lax.cond(on_duty, compute, nothing, columns).astype(jnp.bfloat16)]
    dot_general x2 -> x1, matrix products: 25.7 us -> 10.2 us  [on_device(): lax.dot_general(gathered, columns, (((0,), (0,)), ((), ())), preferred_el...]
  transfers between devices with their start and end apart: 13 -> 4, of which waited for: 12 -> 1; matrix products, arithmetic and copies ran while one was open for 10% -> 1% of each run, Pallas kernels for 0% -> 59%
where the time goes in v1:
time: 420 us; the launch traced here: 416 us
  Pallas kernels  244 us (58%)
  waiting for transfers between devices  137 us (33%)
  between operations  14.1 us (3%)
  matrix products  10.2 us (2%)
  other arithmetic  6.63 us (2%)
    pallas_call x1, Pallas kernels, on_device(): pl.pallas_call(relay, out_shape=(jax.ShapeDtypeStruct((rows, width), BF16...  244 us
    reduce_scatter x1, waiting for transfers between devices, on_device(): lax.psum_scatter(lax.dot_general(gathered, columns, (((0,), (0,)), ((), (...  137 us
    dot_general x1, matrix products, on_device(): lax.dot_general(gathered, columns, (((0,), (0,)), ((), ())), preferred_el...  10.2 us
  transfers between devices with their start and end apart: 4, of which 1 were waited for; matrix products, arithmetic and copies ran while one was open for 1% of the time, Pallas kernels for 59%

profile of v1, /device:TPU:40, one launch (start us, length us, event | category | flops | bytes accessed | tf_op | source)
XLA Modules:
  0.0 415.8 jit_solution(3021425296992794315)
XLA Ops:
  7.2 0.0 reduce-scatter.2.cloned.1.call-start
  7.2 0.1 collective-permute-start
  7.3 2.0 collective-permute-start.1
  9.3 0.1 collective-permute-start.2
  9.4 0.0 copy-start.1
  9.4 244.2 %shard_map.50 = (bf16[128,5120]{1,0:T(8,128)(2,1)}, bf16[512,1280]{1,0:T(8,128)(2,1)}) custom-call(bf16[128,5120]{1,0:T(8,128)(2,1)} %og.1, bf16[5120,1280]{1,0:T(8,128)(2,1)} %bitcast.7), custom_call_target="tpu_custom_call" | custom-call | tf_op jit(solution)/shard_map/pallas_call | solution.py:192
  253.6 0.0 collective-permute-done
  253.6 0.0 copy-done.1
  253.6 2.2 maximum_select_fusion.2
  255.8 0.0 copy-start.2
  255.8 0.0 collective-permute-done.1
  255.8 0.0 collective-permute-done.2
  255.8 1.0 maximum_select_fusion.3
  256.9 0.3 copy-done.2
  257.1 10.2 %convolution_convert_fusion = bf16[5120,1280]{1,0:T(8,128)(2,1)} fusion(bf16[512,1280]{1,0:T(8,128)(2,1)S(1)} %copy-done.2, bf16[256,5120]{1,0:T(8,128)(2,1)S(1)} %maximum_select_fusion.3, bf16[256,5120]{1,0:T(8,128)(2,1)S(1)} %maximum_select_fusion.2, pred[]{:T(512)S(6)} %eq.9), kind=kOutput, calls=%fused_computation | convolution fusion | flops 6741032960 | bytes 19660800 | tf_op jit(solution)/shard_map/dot_general | solution.py:237
  267.3 0.0 reduce-scatter.2.cloned.1.call-update
  267.3 0.0 copy-start
  267.4 137.1 %reduce-scatter.2.cloned.1.call-done = bf16[640,1280]{1,0:T(8,128)(2,1)} async-done(((bf16[5120,1280]{1,0:T(8,128)(2,1)}), bf16[640,1280]{1,0:T(8,128)(2,1)}) %reduce-scatter.2.cloned.1.call-update) | async-done | bytes 1638416 | tf_op jit(solution)/shard_map/reduce_scatter | solution.py:236
  404.5 3.4 bitcast_convert_fusion
  407.9 0.0 copy-done
  407.9 1.1 copy.6
Async XLA Ops:
  7.2 397.3 %reduce-scatter.2.cloned.1.call-start = ((), (), s32[]{:S(2)}) async-start(), calls=%async_computation.1 | async-start | bytes 14745600 | tf_op jit(solution)/shard_map/reduce_scatter | solution.py:236
  7.2 246.4 %collective-permute-start = (bf16[128,5120]{1,0:T(8,128)(2,1)}, bf16[128,5120]{1,0:T(8,128)(2,1)}, u32[]{:S(2)}, u32[]{:S(2)}) collective-permute-start(bf16[128,5120]{1,0:T(8,128)(2,1)} %bitcast.9), channel_id=1, source_target_pairs={{0,1},{1,0},{2,3},{3,2},{4,5},{5,4},{6,7},{7,6},{8,9},{9,8},{10,11... | collective-permute-start | bytes 3932168 | tf_op jit(solution)/shard_map/ppermute | solution.py:228
  7.3 248.5 %collective-permute-start.1 = (bf16[128,5120]{1,0:T(8,128)(2,1)}, bf16[128,5120]{1,0:T(8,128)(2,1)S(1)}, u32[]{:S(2)}, u32[]{:S(2)}) collective-permute-start(bf16[128,5120]{1,0:T(8,128)(2,1)} %bitcast.10), channel_id=1, source_target_pairs={{0,18},{1,19},{2,16},{3,17},{4,22},{5,23},{6,20},{7,21},{8,26},{9,... | collective-permute-start | bytes 3932168 | tf_op jit(solution)/shard_map/ppermute | solution.py:228
  9.3 246.5 %collective-permute-start.2 = (bf16[128,5120]{1,0:T(8,128)(2,1)}, bf16[128,5120]{1,0:T(8,128)(2,1)S(1)}, u32[]{:S(2)}, u32[]{:S(2)}) collective-permute-start(bf16[128,5120]{1,0:T(8,128)(2,1)} %bitcast.11), channel_id=1, source_target_pairs={{0,19},{1,18},{2,17},{3,16},{4,23},{5,22},{6,21},{7,20},{8,27},{9,... | collective-permute-start | bytes 3932168 | tf_op jit(solution)/shard_map/ppermute | solution.py:228
  9.4 244.2 %copy-start.1 = (bf16[1,128,5120]{2,1,0:T(8,128)(2,1)S(1)}, bf16[1,128,5120]{2,1,0:T(8,128)(2,1)}, u32[]{:S(2)}) copy-start(bf16[1,128,5120]{2,1,0:T(8,128)(2,1)} %param.3) | copy-start | bytes 3932164
  255.8 1.3 copy-start.2
  267.3 140.5 %copy-start = (bf16[128,5120]{1,0:T(8,128)(2,1)S(1)}, bf16[128,5120]{1,0:T(8,128)(2,1)}, u32[]{:S(2)}) copy-start(bf16[128,5120]{1,0:T(8,128)(2,1)} %get-tuple-element.4) | copy-start | bytes 3932164
Sparse Core Ops, SparseCore 0:
  267.5 136.9 reduce-scatter.1

commit v2 on v1

v2 whole, which is shorter than its diff:
```python
import jax
import jax.numpy as jnp
from jax import lax
from jax.experimental import pallas as pl
from jax.experimental.pallas import tpu as pltpu
from jax.sharding import PartitionSpec as P

MESH = pl.DeviceIdType.MESH
BF16 = jnp.bfloat16
F32 = jnp.float32
CW = 256
NY = 4
SKEW = 7


def rdma(src, dst, send, recv, dev):
    return pltpu.make_async_remote_copy(
        src_ref=src, dst_ref=dst, send_sem=send, recv_sem=recv, device_id=dev, device_id_type=MESH
    )


def nt_dot(a, b):
    return lax.dot_general(a, b, (((1,), (1,)), ((), ())), preferred_element_type=F32)


def tn_dot(a, b):
    return lax.dot_general(a, b, (((0,), (0,)), ((), ())), preferred_element_type=F32)


def span(start, size):
    return pl.ds(pl.multiple_of(start, 128), size)


def relay(
    og, w, saved,
    out, wg,
    wv, g, ps, pr, own, gn, gy, sv, lo, lr,
    w_sem, w_send, w_recv, gi_send, gi_recv, x_send, x_recv, f_send, f_recv, p_send, p_recv,
    o_send, o_recv, y_send, y_recv, r_send, r_recv, s_send, s_recv, t_send, t_recv, l_send, l_recv, loc, yloc,
):
    rows, width = og.shape
    quarter, half = width // 4, width // 2
    nk = quarter // CW
    pieces = 4
    total = pieces * nk
    block = quarter // 2
    sections = lax.axis_size("section")
    s, d, t = lax.axis_index("section"), lax.axis_index("dp"), lax.axis_index("tensor")
    l, y = d // NY, d % NY
    h, c = t // 2, t % 2
    partner_t = h * 2 + 1 - c
    pair_t = (1 - h) * 2 + c
    cross_t = (1 - h) * 2 + 1 - c
    pair_l = (1 - l) * NY
    partner = (s, d, partner_t)
    pair = (s, pair_l + y, pair_t)
    cross = (s, pair_l + y, cross_t)
    level = (s, pair_l + y, t)
    up = (lax.rem(s + sections - 1, sections), d, t)
    down = (lax.rem(s + 1, sections), d, t)
    first = s == sections - 1
    ys = [lax.rem(y + dy, NY) for dy in range(NY)]
    along = [(s, l * NY + ys[dy], t) for dy in range(NY)]
    pair_along = [(s, pair_l + ys[dy], pair_t) for dy in range(NY)]

    barrier = pltpu.get_barrier_semaphore()
    friends = [partner, pair, cross, level, up, down] + along[1:] + pair_along[1:]
    for dev in friends:
        pl.semaphore_signal(barrier, inc=1, device_id=dev, device_id_type=MESH)
    pl.semaphore_wait(barrier, len(friends))

    cols = span(c * quarter, quarter)
    t_cols = span(t * quarter, quarter)
    own_rows = span(t * rows, rows)
    pair_rows = span(pair_t * rows, rows)
    my_half = span(h * half, half)
    other_half = span((1 - h) * half, half)

    g_pair = rdma(og.at[:, other_half], g.at[own_rows, :], gi_send.at[0], gi_recv.at[0], pair)
    g_partner = rdma(og.at[:, my_half], g.at[own_rows, :], gi_send.at[1], gi_recv.at[1], partner)
    g_fwd = rdma(g.at[pair_rows, :], g.at[pair_rows, :], gi_send.at[2], gi_recv.at[2], partner)

    @pl.when(first)
    def _():
        g_pair.start()
        g_partner.start()

    def w_rows(a, core):
        hh = (1 - h) if a == 0 else h
        return span(hh * half + core * quarter, quarter)

    w_local = [pltpu.make_async_copy(w.at[w_rows(a, c), :], wv.at[a, :, cols], w_sem.at[a]) for a in range(2)]
    w_away = [rdma(w.at[w_rows(a, 1 - c), :], wv.at[a, :, cols], w_send.at[a], w_recv.at[a], partner) for a in range(2)]
    for a in range(2):
        w_away[a].start()
        w_local[a].start()

    def s_copy(chip, dy, b):
        src = saved.at[:, span(b * half + ys[dy] * block, block)]
        dst = sv.at[y, t, :, pl.ds(b * block, block)]
        if chip == 0 and dy == 0:
            return pltpu.make_async_copy(src, dst, s_recv.at[0, y, b])
        dev = along[dy] if chip == 0 else pair_along[dy]
        return rdma(src, dst, s_send.at[chip, dy, b], s_recv.at[chip, y, b], dev)

    def s_start(chip, dys):
        for dy in dys:
            for b in range(2):
                s_copy(chip, dy, b).start()

    s_start(0, range(NY))

    @pl.when(s < sections - 1)
    def _():
        s_start(1, (1, 2, 3))

    @pl.when(s < sections - 2)
    def _():
        s_start(1, (0,))

    def piece_rows(i):
        return span(i * rows, rows)

    def at(j):
        i, k = j // nk, j % nk
        return piece_rows(i), k * CW

    def x_copy(j):
        r, k = at(j)
        return rdma(gn.at[r, span(k, CW)], g.at[r, span(c * quarter + k, CW)], x_send.at[j], x_recv.at[j], up)

    def f_copy(j):
        r, k = at(j)
        here = g.at[r, span(c * quarter + k, CW)]
        return rdma(here, here, f_send.at[j], f_recv.at[j], partner)

    def p_copy(j):
        return rdma(ps.at[j], pr.at[j], p_send.at[j], p_recv.at[j], pair)

    def y_copy(i, side):
        r = piece_rows(i)
        dev = along[1] if side == 0 else along[NY - 1]
        return rdma(g.at[r, cols], gy.at[y, r, :], y_send.at[side, i], y_recv.at[side, i], dev)

    def y_keep(i):
        r = piece_rows(i)
        return pltpu.make_async_copy(g.at[r, cols], gy.at[y, r, :], yloc.at[i])

    def r_copy(i, side):
        here = gy.at[ys[NY - 1] if side == 0 else ys[1], piece_rows(i), pl.ds(side * block, block)]
        dev = along[1] if side == 0 else along[NY - 1]
        return rdma(here, here, r_send.at[side, i], r_recv.at[side, i], dev)

    def pass_on(i):
        for side in range(2):
            y_copy(i, side).wait_recv()
            r_copy(i, side).start()

    @pl.when(first)
    def _():
        here = pltpu.make_async_copy(og.at[:, my_half], g.at[own_rows, :], loc.at[0])
        here.start()
        g_pair.wait_recv()
        g_fwd.start()
        here.wait()
        g_partner.wait_recv()
        g_fwd.wait_recv()
        g_pair.wait_send()
        g_partner.wait_send()
        g_fwd.wait_send()

    def step(j, carry):
        i, k = j // nk, j % nk

        @pl.when(jnp.logical_and(j < total, jnp.logical_not(first)))
        def _():
            x_copy(j).wait_recv()
            f_copy(j).start()

        @pl.when(j >= SKEW)
        def _():
            f = j - SKEW
            r, kk = at(f)
            p_copy(f).wait_recv()
            summed = own[f] + pr[f].astype(F32) + g[r, span(c * quarter + kk, CW)].astype(F32)
            gn[r, span(kk, CW)] = summed.astype(BF16)

            @pl.when(s > 0)
            def _():
                x_copy(f).start()

        @pl.when(jnp.logical_and(j < total, k == nk - 1))
        def _():
            @pl.when(jnp.logical_not(first))
            def _():
                def forwarded(q, carry):
                    f_copy(i * nk + q).wait_recv()
                    return carry

                lax.fori_loop(0, nk, forwarded, 0)

            @pl.when(i == 0)
            def _():
                w_local[0].wait()
                w_away[0].wait_recv()

            def send_part(q, carry):
                f = i * nk + q
                ps[f] = nt_dot(g[piece_rows(i), :], wv[0, span(q * CW, CW), :]).astype(BF16)
                p_copy(f).start()
                return carry

            lax.fori_loop(0, nk, send_part, 0)
            for side in range(2):
                y_copy(i, side).start()
            y_keep(i).start()

            @pl.when(i == 0)
            def _():
                w_local[1].wait()
                w_away[1].wait_recv()

            @pl.when(i >= 2)
            def _():
                pass_on(i - 2)

        @pl.when(jnp.logical_and(j >= nk, j < total + nk))
        def _():
            f = j - nk
            r, kk = at(f)
            own[f] = nt_dot(g[r, :], wv[1, span(kk, CW), :])

        return carry

    lax.fori_loop(0, total + SKEW, step, 0)

    @pl.when(s == sections - 1)
    def _():
        s_start(1, (1, 2, 3))

    @pl.when(s >= sections - 2)
    def _():
        s_start(1, (0,))

    homes = [partner, pair, cross]
    blocks = [partner_t, pair_t, cross_t]
    home = [
        rdma(gn.at[span(b * rows, rows), :], out.at[:, t_cols], o_send.at[i], o_recv.at[i], dev)
        for i, (dev, b) in enumerate(zip(homes, blocks))
    ]
    for copy in home:
        copy.start()
    mine = pltpu.make_async_copy(gn.at[own_rows, :], out.at[:, t_cols], loc.at[0])
    mine.start()

    pass_on(2)
    pass_on(3)

    for chip in range(2):
        for yy in range(NY):
            for b in range(2):
                where = sv.at[yy, 0, :, pl.ds(b * block, block)]
                pltpu.make_async_copy(where, where, s_recv.at[chip, yy, b]).wait()
    tokens = [sv.at[:, c], sv.at[:, 2 + c]]
    across = [rdma(ref, ref, t_send.at[i], t_recv.at[i], partner) for i, ref in enumerate(tokens)]
    for copy in across:
        copy.start()
    for i in range(pieces):
        y_keep(i).wait()
        for side in range(2):
            r_copy(i, side).wait_recv()
    for copy in across:
        copy.wait_recv()

    def l_copy(k):
        return rdma(lo.at[k], lr.at[k], l_send.at[k], l_recv.at[k], level)

    def wgrad(b, k):
        left = sv[:, :, :, span(b * block, block)].reshape(NY * 4 * rows, block)
        right = gy[:, :, span(k * CW, CW)].reshape(NY * 4 * rows, CW)
        return tn_dot(left, right)

    def l_part(k, carry):
        lo[k] = wgrad(1 - l, k).astype(BF16)
        l_copy(k).start()
        return carry

    lax.fori_loop(0, nk, l_part, 0)

    def l_own(k, carry):
        wg[:, span(k * CW, CW)] = wgrad(l, k)
        return carry

    lax.fori_loop(0, nk, l_own, 0)

    def l_sum(k, carry):
        l_copy(k).wait_recv()
        wg[:, span(k * CW, CW)] = wg[:, span(k * CW, CW)] + lr[k].astype(F32)
        return carry

    lax.fori_loop(0, nk, l_sum, 0)

    mine.wait()
    for copy in home:
        copy.wait_recv()
        copy.wait_send()
    for copy in across:
        copy.wait_send()
    for a in range(2):
        w_away[a].wait_send()
    for i in range(pieces):
        for side in range(2):
            y_copy(i, side).wait_send()
            r_copy(i, side).wait_send()
    for chip in range(2):
        for dy in range(NY):
            for b in range(2):
                if chip or dy:
                    s_copy(chip, dy, b).wait_send()

    def drain(j, carry):
        p_copy(j).wait_send()

        @pl.when(s > 0)
        def _():
            x_copy(j).wait_send()

        @pl.when(jnp.logical_not(first))
        def _():
            f_copy(j).wait_send()

        return carry

    lax.fori_loop(0, total, drain, 0)

    def l_drain(k, carry):
        l_copy(k).wait_send()
        return carry

    lax.fori_loop(0, nk, l_drain, 0)


def on_device(saved, weight, out_grad):
    rows, width = out_grad.shape
    quarter, half = width // 4, width // 2
    nk = quarter // CW
    total = 4 * nk
    dma = pltpu.SemaphoreType.DMA
    vmem = pltpu.VMEM
    inside = pl.BlockSpec(memory_space=pltpu.VMEM)
    anywhere = pl.BlockSpec(memory_space=pl.ANY)
    own_input, weight_grad = pl.pallas_call(
        relay,
        out_shape=(
            jax.ShapeDtypeStruct((rows, width), BF16),
            jax.ShapeDtypeStruct((quarter // 2, quarter), F32),
        ),
        in_specs=[inside, anywhere, anywhere],
        out_specs=(inside, inside),
        scratch_shapes=[
            vmem((2, quarter, half), BF16),
            vmem((4 * rows, half), BF16),
            vmem((total, rows, CW), BF16),
            vmem((total, rows, CW), BF16),
            vmem((total, rows, CW), F32),
            vmem((4 * rows, quarter), BF16),
            vmem((NY, 4 * rows, quarter), BF16),
            vmem((NY, 4, rows, quarter), BF16),
            vmem((nk, quarter // 2, CW), BF16),
            vmem((nk, quarter // 2, CW), BF16),
            dma((2,)), dma((2,)), dma((2,)), dma((3,)), dma((3,)),
            dma((total,)), dma((total,)), dma((total,)), dma((total,)), dma((total,)), dma((total,)),
            dma((3,)), dma((3,)), dma((2, 4)), dma((2, 4)), dma((2, 4)), dma((2, 4)),
            dma((2, NY, 2)), dma((2, NY, 2)), dma((2,)), dma((2,)), dma((nk,)), dma((nk,)), dma((1,)), dma((4,)),
        ],
        compiler_params=pltpu.CompilerParams(
            collective_id=0, has_side_effects=True, vmem_limit_bytes=60 * 1024 * 1024
        ),
    )(out_grad, weight[0], saved[0])
    return (own_input[None], weight_grad[None])


def solution(mesh):
    placed = (
        P("section", ("dp", "tensor"), None),
        P("section", None, "tensor"),
        P(("dp", "tensor"), None),
    )
    return jax.shard_map(
        on_device,
        mesh=mesh,
        in_specs=placed,
        out_specs=(P("section", ("dp", "tensor"), None), P("section", "dp", "tensor")),
        check_vma=False,
    )
```

time: 420 us -> 180 us (0.43)
  waiting for transfers between devices: 137 us -> 0 us
  Pallas kernels: 244 us -> 173 us
  between operations: 14.1 us -> 0.64 us
  matrix products: 10.2 us -> 0 us
  other arithmetic: 6.63 us -> 0 us
  local copies, waits for them, and re-layouts: 1.32 us -> 6.3 us
    reduce_scatter x1 -> x0, waiting for transfers between devices: 137 us -> none  [on_device(): lax.psum_scatter(lax.dot_general(gathered, columns, (((0,), (0,)), ((), (...]
    pallas_call x1, Pallas kernels: 244 us -> 173 us  [on_device(): pl.pallas_call(relay, out_shape=(jax.ShapeDtypeStruct((rows, width), BF16...]
    dot_general x1 -> x0, matrix products: 10.2 us -> none  [on_device(): lax.dot_general(gathered, columns, (((0,), (0,)), ((), ())), preferred_el...]
    unnamed x7 -> x2, local copies, waits for them, and re-layouts: 1.32 us -> 6.3 us
  transfers between devices with their start and end apart: 4 -> 0, of which waited for: 1 -> 0; matrix products, arithmetic and copies ran while one was open for 1% -> 0% of each run, Pallas kernels for 59% -> 0%
where the time goes in v2:
time: 180 us; the launch traced here: 179 us
  Pallas kernels  173 us (96%)
  local copies, waits for them, and re-layouts  6.3 us (4%)
    pallas_call x1, Pallas kernels, on_device(): pl.pallas_call(relay, out_shape=(jax.ShapeDtypeStruct((rows, width), BF16...  173 us
    unnamed x2, local copies, waits for them, and re-layouts  6.3 us

profile of v2, /device:TPU:40, one launch (start us, length us, event | category | flops | bytes accessed | tf_op | source)
XLA Modules:
  0.0 179.5 jit_solution(4847844109159626852)
XLA Ops:
  0.6 172.6 %shard_map.50 = (bf16[128,5120]{1,0:T(8,128)(2,1)}, f32[640,1280]{1,0:T(8,128)}) custom-call(bf16[128,5120]{1,0:T(8,128)(2,1)} %og.1, bf16[5120,1280]{1,0:T(8,128)(2,1)} %bitcast.4, bf16[128,5120]{1,0:T(8,128)(2,1)} %bitcast.7), custom_call_target="tpu_custom_call" | custom-call | tf_op jit(solution)/shard_map/pallas_call | solution.py:352
  173.2 2.5 %copy.7 = bf16[1,128,5120]{2,1,0:T(8,128)(2,1)} copy(bf16[1,128,5120]{2,1,0:T(8,128)(2,1)} %bitcast.6) | data formatting | bytes 2621440
  175.7 3.8 %copy.8 = f32[1,640,1280]{2,1,0:T(8,128)} copy(f32[1,640,1280]{2,1,0:T(8,128)} %bitcast.5) | data formatting | bytes 6553600

commit v3 on v2

--- a/solution.py
+++ b/solution.py
@@ -35,7 +35,7 @@
     og, w, saved,
     out, wg,
     wv, g, ps, pr, own, gn, gy, sv, lo, lr,
-    w_sem, w_send, w_recv, gi_send, gi_recv, x_send, x_recv, f_send, f_recv, p_send, p_recv,
+    w_sem, w_send, w_recv, gi_send, gi_recv, gf_send, gf_recv, x_send, x_recv, f_send, f_recv, p_send, p_recv,
     o_send, o_recv, y_send, y_recv, r_send, r_recv, s_send, s_recv, t_send, t_recv, l_send, l_recv, loc, yloc,
 ):
     rows, width = og.shape
@@ -76,13 +76,43 @@
     my_half = span(h * half, half)
     other_half = span((1 - h) * half, half)
 
-    g_pair = rdma(og.at[:, other_half], g.at[own_rows, :], gi_send.at[0], gi_recv.at[0], pair)
-    g_partner = rdma(og.at[:, my_half], g.at[own_rows, :], gi_send.at[1], gi_recv.at[1], partner)
-    g_fwd = rdma(g.at[pair_rows, :], g.at[pair_rows, :], gi_send.at[2], gi_recv.at[2], partner)
+    cuts = (0, half * 7 // 20, half * 14 // 20, half)
+
+    def g_there(q):
+        return pl.ds(cuts[q], cuts[q + 1] - cuts[q])
+
+    def g_cols(q):
+        return span((1 - h) * half + cuts[q], cuts[q + 1] - cuts[q])
+
+    def g_fwd(q):
+        here = g.at[pair_rows, g_there(q)]
+        return rdma(here, here, gf_send.at[q], gf_recv.at[q], partner)
+
+    g_pair = rdma(og.at[:, g_cols(0)], g.at[own_rows, g_there(0)], gi_send.at[0], gi_recv.at[0], pair)
+
+    def g_lend(q):
+        there = gn.at[pl.ds(0, rows), pl.ds(0, cuts[q + 1] - cuts[q])]
+        return rdma(og.at[:, g_cols(q)], there, gf_send.at[q], gf_recv.at[q], pair)
+
+    def g_relay(q, dev):
+        here = gn.at[pl.ds(0, rows), pl.ds(0, cuts[q + 1] - cuts[q])]
+        return rdma(here, g.at[pair_rows, g_there(q)], gi_send.at[q], gi_recv.at[q], dev)
+
+    beside = [(1, s == sections - 2, down), (2, s == 0, up)]
 
     @pl.when(first)
     def _():
         g_pair.start()
+
+    for q, lends, dev in beside:
+        @pl.when(lends)
+        def _():
+            g_lend(q).start()
+
+    g_partner = rdma(og.at[:, my_half], g.at[own_rows, :], gi_send.at[3], gi_recv.at[3], partner)
+
+    @pl.when(first)
+    def _():
         g_partner.start()
 
     def w_rows(a, core):
@@ -91,9 +121,19 @@
 
     w_local = [pltpu.make_async_copy(w.at[w_rows(a, c), :], wv.at[a, :, cols], w_sem.at[a]) for a in range(2)]
     w_away = [rdma(w.at[w_rows(a, 1 - c), :], wv.at[a, :, cols], w_send.at[a], w_recv.at[a], partner) for a in range(2)]
-    for a in range(2):
-        w_away[a].start()
-        w_local[a].start()
+    w_away[0].start()
+    w_local[0].start()
+    w_local[1].start()
+
+    @pl.when(jnp.logical_not(first))
+    def _():
+        w_away[1].start()
+
+    for q, lends, dev in beside:
+        @pl.when(lends)
+        def _():
+            g_lend(q).wait_recv()
+            g_relay(q, dev).start()
 
     def s_copy(chip, dy, b):
         src = saved.at[:, span(b * half + ys[dy] * block, block)]
@@ -110,13 +150,9 @@
 
     s_start(0, range(NY))
 
-    @pl.when(s < sections - 1)
-    def _():
-        s_start(1, (1, 2, 3))
-
     @pl.when(s < sections - 2)
     def _():
-        s_start(1, (0,))
+        s_start(1, range(NY))
 
     def piece_rows(i):
         return span(i * rows, rows)
@@ -161,13 +197,40 @@
         here = pltpu.make_async_copy(og.at[:, my_half], g.at[own_rows, :], loc.at[0])
         here.start()
         g_pair.wait_recv()
-        g_fwd.start()
+        g_fwd(0).start()
+        for q, lends, dev in beside:
+            g_relay(q, dev).wait_recv()
+            g_fwd(q).start()
+        w_away[1].start()
         here.wait()
         g_partner.wait_recv()
-        g_fwd.wait_recv()
+        g_partner.wait_send()
         g_pair.wait_send()
-        g_partner.wait_send()
-        g_fwd.wait_send()
+        for q in range(3):
+            g_fwd(q).wait_recv()
+            g_fwd(q).wait_send()
+
+    for q, lends, dev in beside:
+        @pl.when(lends)
+        def _():
+            g_lend(q).wait_send()
+            g_relay(q, dev).wait_send()
+
+    tokens = [sv.at[:, c], sv.at[:, 2 + c]]
+    across = [rdma(ref, ref, t_send.at[i], t_recv.at[i], partner) for i, ref in enumerate(tokens)]
+
+    def s_across():
+        for chip in range(2):
+            for yy in range(NY):
+                for b in range(2):
+                    where = sv.at[yy, 0, :, pl.ds(b * block, block)]
+                    pltpu.make_async_copy(where, where, s_recv.at[chip, yy, b]).wait()
+        for copy in across:
+            copy.start()
+
+    @pl.when(s == 0)
+    def _():
+        s_across()
 
     def step(j, carry):
         i, k = j // nk, j % nk
@@ -191,6 +254,10 @@
 
         @pl.when(jnp.logical_and(j < total, k == nk - 1))
         def _():
+            for side in range(2):
+                y_copy(i, side).start()
+            y_keep(i).start()
+
             @pl.when(jnp.logical_not(first))
             def _():
                 def forwarded(q, carry):
@@ -211,9 +278,6 @@
                 return carry
 
             lax.fori_loop(0, nk, send_part, 0)
-            for side in range(2):
-                y_copy(i, side).start()
-            y_keep(i).start()
 
             @pl.when(i == 0)
             def _():
@@ -224,6 +288,14 @@
             def _():
                 pass_on(i - 2)
 
+        @pl.when(j == total)
+        def _():
+            pass_on(2)
+
+        @pl.when(j == total + 4)
+        def _():
+            pass_on(3)
+
         @pl.when(jnp.logical_and(j >= nk, j < total + nk))
         def _():
             f = j - nk
@@ -234,13 +306,9 @@
 
     lax.fori_loop(0, total + SKEW, step, 0)
 
-    @pl.when(s == sections - 1)
-    def _():
-        s_start(1, (1, 2, 3))
-
     @pl.when(s >= sections - 2)
     def _():
-        s_start(1, (0,))
+        s_start(1, range(NY))
 
     homes = [partner, pair, cross]
     blocks = [partner_t, pair_t, cross_t]
@@ -253,18 +321,11 @@
     mine = pltpu.make_async_copy(gn.at[own_rows, :], out.at[:, t_cols], loc.at[0])
     mine.start()
 
-    pass_on(2)
-    pass_on(3)
-
-    for chip in range(2):
-        for yy in range(NY):
-            for b in range(2):
-                where = sv.at[yy, 0, :, pl.ds(b * block, block)]
-                pltpu.make_async_copy(where, where, s_recv.at[chip, yy, b]).wait()
-    tokens = [sv.at[:, c], sv.at[:, 2 + c]]
-    across = [rdma(ref, ref, t_send.at[i], t_recv.at[i], partner) for i, ref in enumerate(tokens)]
-    for copy in across:
-        copy.start()
+
+    @pl.when(s > 0)
+    def _():
+        s_across()
+
     for i in range(pieces):
         y_keep(i).wait()
         for side in range(2):
@@ -368,13 +429,13 @@
             vmem((NY, 4, rows, quarter), BF16),
             vmem((nk, quarter // 2, CW), BF16),
             vmem((nk, quarter // 2, CW), BF16),
-            dma((2,)), dma((2,)), dma((2,)), dma((3,)), dma((3,)),
+            dma((2,)), dma((2,)), dma((2,)), dma((4,)), dma((4,)), dma((3,)), dma((3,)),
             dma((total,)), dma((total,)), dma((total,)), dma((total,)), dma((total,)), dma((total,)),
             dma((3,)), dma((3,)), dma((2, 4)), dma((2, 4)), dma((2, 4)), dma((2, 4)),
             dma((2, NY, 2)), dma((2, NY, 2)), dma((2,)), dma((2,)), dma((nk,)), dma((nk,)), dma((1,)), dma((4,)),
         ],
         compiler_params=pltpu.CompilerParams(
-            collective_id=0, has_side_effects=True, vmem_limit_bytes=60 * 1024 * 1024
+            collective_id=0, has_side_effects=True, vmem_limit_bytes=46 * 1024 * 1024
         ),
     )(out_grad, weight[0], saved[0])
     return (own_input[None], weight_grad[None])

time: 180 us -> 167 us (0.928)
  Pallas kernels: 173 us -> 159 us
    pallas_call x1, Pallas kernels: 173 us -> 159 us  [on_device(): pl.pallas_call(relay, out_shape=(jax.ShapeDtypeStruct((rows, width), BF16...]
    unnamed x2 -> x6, local copies, waits for them, and re-layouts: 6.3 us -> 5.39 us
where the time goes in v3:
time: 167 us; the launch traced here: 165 us
  Pallas kernels  159 us (95%)
  local copies, waits for them, and re-layouts  5.39 us (3%)
    pallas_call x1, Pallas kernels, on_device(): pl.pallas_call(relay, out_shape=(jax.ShapeDtypeStruct((rows, width), BF16...  159 us
    unnamed x6, local copies, waits for them, and re-layouts  5.39 us

profile of v3, /device:TPU:40, one launch (start us, length us, event | category | flops | bytes accessed | tf_op | source)
XLA Modules:
  0.0 165.1 jit_solution(1887920727980445030)
XLA Ops:
  0.6 0.0 copy-start
  0.6 1.3 copy-done
  1.9 0.0 copy-start.1
  1.9 1.3 copy-done.1
  3.3 159.1 %shard_map.50 = (bf16[128,5120]{1,0:T(8,128)(2,1)S(1)}, f32[640,1280]{1,0:T(8,128)S(1)}) custom-call(bf16[128,5120]{1,0:T(8,128)(2,1)S(1)} %copy-done, bf16[5120,1280]{1,0:T(8,128)(2,1)} %bitcast.7, bf16[128,5120]{1,0:T(8,128)(2,1)S(1)} %bitcast.6), custom_call_target="tpu_custom_call" | custom-call | tf_op jit(solution)/shard_map/pallas_call | solution.py:413
  162.4 1.1 copy.7
  163.4 1.7 %copy.8 = f32[1,640,1280]{2,1,0:T(8,128)} copy(f32[1,640,1280]{2,1,0:T(8,128)S(1)} %bitcast.4) | data formatting | bytes 6553600
Async XLA Ops:
  0.6 1.3 copy-start
  1.9 1.3 copy-start.1

commit v4 on v3

--- a/solution.py
+++ b/solution.py
@@ -34,9 +34,10 @@
 def relay(
     og, w, saved,
     out, wg,
-    wv, g, ps, pr, own, gn, gy, sv, lo, lr,
+    wv, g, ps, pr, own, gn, gy, sv, lo, lr, sv2, lo2, lr2,
     w_sem, w_send, w_recv, gi_send, gi_recv, gf_send, gf_recv, x_send, x_recv, f_send, f_recv, p_send, p_recv,
     o_send, o_recv, y_send, y_recv, r_send, r_recv, s_send, s_recv, t_send, t_recv, l_send, l_recv, loc, yloc,
+    y2_send, y2_recv, g2_send, g2_recv, u_send, u_recv, v_send, v_recv, m_send, m_recv,
 ):
     rows, width = og.shape
     quarter, half = width // 4, width // 2
@@ -150,9 +151,13 @@
 
     s_start(0, range(NY))
 
+    @pl.when(s < sections - 1)
+    def _():
+        s_start(1, (1, 2))
+
     @pl.when(s < sections - 2)
     def _():
-        s_start(1, range(NY))
+        s_start(1, (0, 3))
 
     def piece_rows(i):
         return span(i * rows, rows)
@@ -186,6 +191,57 @@
         here = gy.at[ys[NY - 1] if side == 0 else ys[1], piece_rows(i), pl.ds(side * block, block)]
         dev = along[1] if side == 0 else along[NY - 1]
         return rdma(here, here, r_send.at[side, i], r_recv.at[side, i], dev)
+
+    last = s == 0
+    l_half = span(c * quarter + l * block, block)
+    near, far = pl.ds(0, block), pl.ds(block, block)
+
+    def g2_copy(i):
+        r = piece_rows(i)
+        return rdma(
+            g.at[r, span(c * quarter + (1 - l) * block, block)], gy.at[y, r, far], g2_send.at[i], g2_recv.at[i], level
+        )
+
+    def y0_copy(i, side):
+        r = piece_rows(i)
+        dev = along[1] if side == 0 else along[NY - 1]
+        return rdma(g.at[r, l_half], gy.at[y, r, near], y_send.at[side, i], y_recv.at[side, i], dev)
+
+    def y2_copy(i, side):
+        here = gy.at[y, piece_rows(i), far]
+        dev = along[1] if side == 0 else along[NY - 1]
+        return rdma(here, here, y2_send.at[side, i], y2_recv.at[side, i], dev)
+
+    def y0_keep(i):
+        r = piece_rows(i)
+        return pltpu.make_async_copy(g.at[r, l_half], gy.at[y, r, near], yloc.at[i])
+
+    def spread(i):
+        @pl.when(last)
+        def _():
+            g2_copy(i).start()
+            for side in range(2):
+                y0_copy(i, side).start()
+            y0_keep(i).start()
+
+        @pl.when(jnp.logical_not(last))
+        def _():
+            for side in range(2):
+                y_copy(i, side).start()
+            y_keep(i).start()
+
+    def spread_far(i):
+        g2_copy(i).wait_recv()
+        for side in range(2):
+            y2_copy(i, side).start()
+
+    def pass_near(i):
+        y0_copy(i, 0).wait_recv()
+        r_copy(i, 0).start()
+
+    def pass_far(i):
+        y2_copy(i, 1).wait_recv()
+        r_copy(i, 1).start()
 
     def pass_on(i):
         for side in range(2):
@@ -219,17 +275,29 @@
     tokens = [sv.at[:, c], sv.at[:, 2 + c]]
     across = [rdma(ref, ref, t_send.at[i], t_recv.at[i], partner) for i, ref in enumerate(tokens)]
 
+    def s_arrived(chip):
+        for yy in range(NY):
+            for b in range(2):
+                where = sv.at[yy, 0, :, pl.ds(b * block, block)]
+                pltpu.make_async_copy(where, where, s_recv.at[chip, yy, b]).wait()
+
     def s_across():
-        for chip in range(2):
-            for yy in range(NY):
-                for b in range(2):
-                    where = sv.at[yy, 0, :, pl.ds(b * block, block)]
-                    pltpu.make_async_copy(where, where, s_recv.at[chip, yy, b]).wait()
         for copy in across:
             copy.start()
 
-    @pl.when(s == 0)
-    def _():
+    beyond = [(sv.at[:, t], sv2.at[:, t]), (sv.at[:, pair_t], sv2.at[:, pair_t])]
+    lent = [rdma(*beyond[0], u_send.at[0], u_recv.at[0], level)] + [
+        rdma(sv.at[yy, pair_t], sv2.at[yy, pair_t], u_send.at[1 + yy], u_recv.at[1 + yy], level) for yy in range(NY)
+    ]
+    across2 = [rdma(dst, dst, v_send.at[i], v_recv.at[i], partner) for i, (src, dst) in enumerate(beyond)]
+
+    @pl.when(last)
+    def _():
+        s_arrived(0)
+        lent[0].start()
+        s_arrived(1)
+        lent[1].start()
+        lent[2].start()
         s_across()
 
     def step(j, carry):
@@ -254,9 +322,15 @@
 
         @pl.when(jnp.logical_and(j < total, k == nk - 1))
         def _():
-            for side in range(2):
-                y_copy(i, side).start()
-            y_keep(i).start()
+            spread(i)
+            for q in range(2):
+                @pl.when(jnp.logical_and(last, i == q))
+                def _():
+                    lent[3 + q].start()
+
+            @pl.when(jnp.logical_and(last, i > 0))
+            def _():
+                pass_near(i - 1)
 
             @pl.when(jnp.logical_not(first))
             def _():
@@ -284,17 +358,48 @@
                 w_local[1].wait()
                 w_away[1].wait_recv()
 
+            @pl.when(jnp.logical_and(last, i == 3))
+            def _():
+                for copy in lent:
+                    copy.wait_recv()
+                for on in across2:
+                    on.start()
+
+            @pl.when(jnp.logical_and(jnp.logical_not(last), i >= 2))
+            def _():
+                pass_on(i - 2)
+
+        @pl.when(jnp.logical_and(last, jnp.logical_and(j < total, k == nk - 2)))
+        def _():
+            @pl.when(i >= 1)
+            def _():
+                spread_far(i - 1)
+
             @pl.when(i >= 2)
             def _():
-                pass_on(i - 2)
+                pass_far(i - 2)
 
         @pl.when(j == total)
         def _():
-            pass_on(2)
+            @pl.when(last)
+            def _():
+                spread_far(pieces - 1)
+                pass_far(pieces - 2)
+                pass_near(pieces - 1)
+
+            @pl.when(jnp.logical_not(last))
+            def _():
+                pass_on(pieces - 2)
 
         @pl.when(j == total + 4)
         def _():
-            pass_on(3)
+            @pl.when(last)
+            def _():
+                pass_far(pieces - 1)
+
+            @pl.when(jnp.logical_not(last))
+            def _():
+                pass_on(pieces - 1)
 
         @pl.when(jnp.logical_and(j >= nk, j < total + nk))
         def _():
@@ -306,9 +411,13 @@
 
     lax.fori_loop(0, total + SKEW, step, 0)
 
+    @pl.when(s == sections - 1)
+    def _():
+        s_start(1, (1, 2))
+
     @pl.when(s >= sections - 2)
     def _():
-        s_start(1, range(NY))
+        s_start(1, (0, 3))
 
     homes = [partner, pair, cross]
     blocks = [partner_t, pair_t, cross_t]
@@ -324,10 +433,25 @@
 
     @pl.when(s > 0)
     def _():
+        for chip in range(2):
+            s_arrived(chip)
         s_across()
 
+    @pl.when(last)
+    def _():
+        for i in range(pieces):
+            y0_keep(i).wait()
+            y0_copy(i, 1).wait_recv()
+            y2_copy(i, 0).wait_recv()
+        for on in across2:
+            on.wait_recv()
+
+    @pl.when(jnp.logical_not(last))
+    def _():
+        for i in range(pieces):
+            y_keep(i).wait()
+
     for i in range(pieces):
-        y_keep(i).wait()
         for side in range(2):
             r_copy(i, side).wait_recv()
     for copy in across:
@@ -346,20 +470,49 @@
         l_copy(k).start()
         return carry
 
-    lax.fori_loop(0, nk, l_part, 0)
-
     def l_own(k, carry):
         wg[:, span(k * CW, CW)] = wgrad(l, k)
         return carry
-
-    lax.fori_loop(0, nk, l_own, 0)
 
     def l_sum(k, carry):
         l_copy(k).wait_recv()
         wg[:, span(k * CW, CW)] = wg[:, span(k * CW, CW)] + lr[k].astype(F32)
         return carry
 
-    lax.fori_loop(0, nk, l_sum, 0)
+    parts = ((0, 128), (128, 256), (384, 256))
+
+    def m_copy(k):
+        here = pl.ds(*parts[k])
+        return rdma(lo2.at[:, here], lr2.at[:, here], m_send.at[k], m_recv.at[k], level)
+
+    def both(b, k):
+        at, wide = parts[k]
+
+        def part(ref, start):
+            left = ref[:, :, :, span(b * block, block)].reshape(NY * 4 * rows, block)
+            return tn_dot(left, gy[:, :, pl.ds(start + at, wide)].reshape(NY * 4 * rows, wide))
+
+        return part(sv, 0) + part(sv2, block)
+
+    def m_all():
+        for k, (at, wide) in enumerate(parts):
+            lo2[:, pl.ds(at, wide)] = both(1 - l, k).astype(BF16)
+            m_copy(k).start()
+        for k, (at, wide) in enumerate(parts):
+            wg[:, span(l * block + at, wide)] = both(l, k)
+        for k, (at, wide) in enumerate(parts):
+            m_copy(k).wait_recv()
+            wg[:, span((1 - l) * block + at, wide)] = lr2[:, pl.ds(at, wide)].astype(F32)
+
+    @pl.when(last)
+    def _():
+        m_all()
+
+    @pl.when(jnp.logical_not(last))
+    def _():
+        lax.fori_loop(0, nk, l_part, 0)
+        lax.fori_loop(0, nk, l_own, 0)
+        lax.fori_loop(0, nk, l_sum, 0)
 
     mine.wait()
     for copy in home:
@@ -371,8 +524,27 @@
         w_away[a].wait_send()
     for i in range(pieces):
         for side in range(2):
-            y_copy(i, side).wait_send()
             r_copy(i, side).wait_send()
+
+    @pl.when(last)
+    def _():
+        for i in range(pieces):
+            g2_copy(i).wait_send()
+            for side in range(2):
+                y0_copy(i, side).wait_send()
+                y2_copy(i, side).wait_send()
+        for copy in lent + across2:
+            copy.wait_send()
+        for k in range(len(parts)):
+            m_copy(k).wait_send()
+
+    @pl.when(jnp.logical_not(last))
+    def _():
+        for i in range(pieces):
+            for side in range(2):
+                y_copy(i, side).wait_send()
+        for k in range(nk):
+            l_copy(k).wait_send()
     for chip in range(2):
         for dy in range(NY):
             for b in range(2):
@@ -393,12 +565,6 @@
         return carry
 
     lax.fori_loop(0, total, drain, 0)
-
-    def l_drain(k, carry):
-        l_copy(k).wait_send()
-        return carry
-
-    lax.fori_loop(0, nk, l_drain, 0)
 
 
 def on_device(saved, weight, out_grad):
@@ -429,13 +595,18 @@
             vmem((NY, 4, rows, quarter), BF16),
             vmem((nk, quarter // 2, CW), BF16),
             vmem((nk, quarter // 2, CW), BF16),
+            vmem((NY, 4, rows, quarter), BF16),
+            vmem((quarter // 2, quarter // 2), BF16),
+            vmem((quarter // 2, quarter // 2), BF16),
             dma((2,)), dma((2,)), dma((2,)), dma((4,)), dma((4,)), dma((3,)), dma((3,)),
             dma((total,)), dma((total,)), dma((total,)), dma((total,)), dma((total,)), dma((total,)),
             dma((3,)), dma((3,)), dma((2, 4)), dma((2, 4)), dma((2, 4)), dma((2, 4)),
             dma((2, NY, 2)), dma((2, NY, 2)), dma((2,)), dma((2,)), dma((nk,)), dma((nk,)), dma((1,)), dma((4,)),
+            dma((2, 4)), dma((2, 4)), dma((4,)), dma((4,)), dma((5,)), dma((5,)), dma((2,)), dma((2,)),
+            dma((3,)), dma((3,)),
         ],
         compiler_params=pltpu.CompilerParams(
-            collective_id=0, has_side_effects=True, vmem_limit_bytes=46 * 1024 * 1024
+            collective_id=0, has_side_effects=True, vmem_limit_bytes=50 * 1024 * 1024
         ),
     )(out_grad, weight[0], saved[0])
     return (own_input[None], weight_grad[None])

time: 167 us -> 161 us (0.964)
  Pallas kernels: 159 us -> 151 us
  local copies, waits for them, and re-layouts: 5.39 us -> 7.53 us
    pallas_call x1, Pallas kernels: 159 us -> 151 us  [on_device(): pl.pallas_call(relay, out_shape=(jax.ShapeDtypeStruct((rows, width), BF16...]
    unnamed x6, local copies, waits for them, and re-layouts: 5.39 us -> 7.53 us
where the time goes in v4:
time: 161 us; the launch traced here: 159 us
  Pallas kernels  151 us (94%)
  local copies, waits for them, and re-layouts  7.53 us (5%)
    pallas_call x1, Pallas kernels, on_device(): pl.pallas_call(relay, out_shape=(jax.ShapeDtypeStruct((rows, width), BF16...  151 us
    unnamed x6, local copies, waits for them, and re-layouts  7.53 us

profile of v4, /device:TPU:40, one launch (start us, length us, event | category | flops | bytes accessed | tf_op | source)
XLA Modules:
  0.0 159.1 jit_solution(12373683019057919135)
XLA Ops:
  0.6 0.0 copy-start
  0.6 1.3 copy-done
  1.9 0.0 copy-start.1
  1.9 1.3 copy-done.1
  3.3 151.0 %shard_map.50 = (bf16[128,5120]{1,0:T(8,128)(2,1)S(1)}, f32[640,1280]{1,0:T(8,128)}) custom-call(bf16[128,5120]{1,0:T(8,128)(2,1)S(1)} %copy-done, bf16[5120,1280]{1,0:T(8,128)(2,1)} %bitcast.6, bf16[128,5120]{1,0:T(8,128)(2,1)S(1)} %bitcast.5), custom_call_target="tpu_custom_call" | custom-call | tf_op jit(solution)/shard_map/pallas_call | solution.py:579
  154.2 1.1 copy.7
  155.3 3.8 %copy.8 = f32[1,640,1280]{2,1,0:T(8,128)} copy(f32[1,640,1280]{2,1,0:T(8,128)} %bitcast.7) | data formatting | bytes 6553600
Async XLA Ops:
  0.6 1.3 copy-start
  1.9 1.3 copy-start.1

commit v5 on v4

--- a/solution.py
+++ b/solution.py
@@ -567,6 +567,17 @@
     lax.fori_loop(0, total, drain, 0)
 
 
+def put_out(own_input, weight_grad, inputs_out, weights_out, sems):
+    copies = [
+        pltpu.make_async_copy(own_input, inputs_out.at[0], sems.at[0]),
+        pltpu.make_async_copy(weight_grad, weights_out.at[0], sems.at[1]),
+    ]
+    for copy in copies:
+        copy.start()
+    for copy in copies:
+        copy.wait()
+
+
 def on_device(saved, weight, out_grad):
     rows, width = out_grad.shape
     quarter, half = width // 4, width // 2
@@ -575,14 +586,15 @@
     dma = pltpu.SemaphoreType.DMA
     vmem = pltpu.VMEM
     inside = pl.BlockSpec(memory_space=pltpu.VMEM)
+    outside = pl.BlockSpec(memory_space=pltpu.HBM)
     anywhere = pl.BlockSpec(memory_space=pl.ANY)
     own_input, weight_grad = pl.pallas_call(
         relay,
         out_shape=(
-            jax.ShapeDtypeStruct((rows, width), BF16),
-            jax.ShapeDtypeStruct((quarter // 2, quarter), F32),
+            vmem((rows, width), BF16),
+            vmem((quarter // 2, quarter), F32),
         ),
-        in_specs=[inside, anywhere, anywhere],
+        in_specs=[outside, outside, outside],
         out_specs=(inside, inside),
         scratch_shapes=[
             vmem((2, quarter, half), BF16),
@@ -609,7 +621,17 @@
             collective_id=0, has_side_effects=True, vmem_limit_bytes=50 * 1024 * 1024
         ),
     )(out_grad, weight[0], saved[0])
-    return (own_input[None], weight_grad[None])
+    return pl.pallas_call(
+        put_out,
+        out_shape=(
+            jax.ShapeDtypeStruct((1, rows, width), BF16),
+            jax.ShapeDtypeStruct((1, quarter // 2, quarter), F32),
+        ),
+        in_specs=[inside, inside],
+        out_specs=(outside, outside),
+        scratch_shapes=[dma((2,))],
+        compiler_params=pltpu.CompilerParams(vmem_limit_bytes=6 * 1024 * 1024),
+    )(own_input, weight_grad)
 
 
 def solution(mesh):

time: 161 us -> 155 us (0.963)
  local copies, waits for them, and re-layouts: 7.53 us -> 0 us
    unnamed x6 -> x0, local copies, waits for them, and re-layouts: 7.53 us -> none
    pallas_call x1 -> x2, Pallas kernels: 151 us -> 152 us  [the longest x1 150 us: on_device(): pl.pallas_call(relay, out_shape=(vmem((rows, width), BF16), vmem((quarter...]
where the time goes in v5:
time: 155 us; the launch traced here: 153 us
  Pallas kernels  152 us (98%)
    pallas_call x1, Pallas kernels, on_device(): pl.pallas_call(relay, out_shape=(vmem((rows, width), BF16), vmem((quarter...  150 us

profile of v5, /device:TPU:40, one launch (start us, length us, event | category | flops | bytes accessed | tf_op | source)
XLA Modules:
  0.0 152.8 jit_solution(18270221241121968308)
XLA Ops:
  0.6 149.8 %shard_map.50 = (bf16[128,5120]{1,0:T(8,128)(2,1)S(1)}, f32[640,1280]{1,0:T(8,128)S(1)}) custom-call(bf16[128,5120]{1,0:T(8,128)(2,1)} %og.1, bf16[5120,1280]{1,0:T(8,128)(2,1)} %bitcast.2, bf16[128,5120]{1,0:T(8,128)(2,1)} %bitcast.3), custom_call_target="tpu_custom_call" | custom-call | tf_op jit(solution)/shard_map/pallas_call | solution.py:591
  150.5 2.2 %shard_map.51 = (bf16[1,128,5120]{2,1,0:T(8,128)(2,1)}, f32[1,640,1280]{2,1,0:T(8,128)}) custom-call(bf16[128,5120]{1,0:T(8,128)(2,1)S(1)} %get-tuple-element.4.own_input, f32[640,1280]{1,0:T(8,128)S(1)} %get-tuple-element.5.weight_grad), custom_call_target="tpu_custom_call" | custom-call | tf_op jit(solution)/shard_map/pallas_call | solution.py:624

commit v6 on v5

--- a/solution.py
+++ b/solution.py
@@ -437,25 +437,22 @@
             s_arrived(chip)
         s_across()
 
+    for copy in across:
+        copy.wait_recv()
+
     @pl.when(last)
     def _():
         for i in range(pieces):
             y0_keep(i).wait()
             y0_copy(i, 1).wait_recv()
-            y2_copy(i, 0).wait_recv()
-        for on in across2:
-            on.wait_recv()
+            r_copy(i, 0).wait_recv()
 
     @pl.when(jnp.logical_not(last))
     def _():
         for i in range(pieces):
             y_keep(i).wait()
-
-    for i in range(pieces):
-        for side in range(2):
-            r_copy(i, side).wait_recv()
-    for copy in across:
-        copy.wait_recv()
+            for side in range(2):
+                r_copy(i, side).wait_recv()
 
     def l_copy(k):
         return rdma(lo.at[k], lr.at[k], l_send.at[k], l_recv.at[k], level)
@@ -485,18 +482,25 @@
         here = pl.ds(*parts[k])
         return rdma(lo2.at[:, here], lr2.at[:, here], m_send.at[k], m_recv.at[k], level)
 
+    def part(ref, start, b, k):
+        at, wide = parts[k]
+        left = ref[:, :, :, span(b * block, block)].reshape(NY * 4 * rows, block)
+        return tn_dot(left, gy[:, :, pl.ds(start + at, wide)].reshape(NY * 4 * rows, wide))
+
     def both(b, k):
-        at, wide = parts[k]
-
-        def part(ref, start):
-            left = ref[:, :, :, span(b * block, block)].reshape(NY * 4 * rows, block)
-            return tn_dot(left, gy[:, :, pl.ds(start + at, wide)].reshape(NY * 4 * rows, wide))
-
-        return part(sv, 0) + part(sv2, block)
+        return part(sv, 0, b, k) + part(sv2, block, b, k)
 
     def m_all():
         for k, (at, wide) in enumerate(parts):
-            lo2[:, pl.ds(at, wide)] = both(1 - l, k).astype(BF16)
+            wg[:, span((1 - l) * block + at, wide)] = part(sv, 0, 1 - l, k)
+        for on in across2:
+            on.wait_recv()
+        for i in range(pieces):
+            y2_copy(i, 0).wait_recv()
+            r_copy(i, 1).wait_recv()
+        for k, (at, wide) in enumerate(parts):
+            near_sum = wg[:, span((1 - l) * block + at, wide)]
+            lo2[:, pl.ds(at, wide)] = (near_sum + part(sv2, block, 1 - l, k)).astype(BF16)
             m_copy(k).start()
         for k, (at, wide) in enumerate(parts):
             wg[:, span(l * block + at, wide)] = both(l, k)

time: 155 us -> 154 us (level); the launches traced: 153 us -> 154 us
  no operation moved by 1% of the time
where the time goes in v6:
time: 154 us
  Pallas kernels  153 us (99%)
    pallas_call x1, Pallas kernels, on_device(): pl.pallas_call(relay, out_shape=(vmem((rows, width), BF16), vmem((quarter...  151 us

profile of v6, /device:TPU:40, one launch (start us, length us, event | category | flops | bytes accessed | tf_op | source)
XLA Modules:
  0.0 153.6 jit_solution(7906210172662338288)
XLA Ops:
  0.6 150.7 %shard_map.50 = (bf16[128,5120]{1,0:T(8,128)(2,1)S(1)}, f32[640,1280]{1,0:T(8,128)S(1)}) custom-call(bf16[128,5120]{1,0:T(8,128)(2,1)} %og.1, bf16[5120,1280]{1,0:T(8,128)(2,1)} %bitcast.2, bf16[128,5120]{1,0:T(8,128)(2,1)} %bitcast.3), custom_call_target="tpu_custom_call" | custom-call | tf_op jit(solution)/shard_map/pallas_call | solution.py:595
  151.3 2.2 %shard_map.51 = (bf16[1,128,5120]{2,1,0:T(8,128)(2,1)}, f32[1,640,1280]{2,1,0:T(8,128)}) custom-call(bf16[128,5120]{1,0:T(8,128)(2,1)S(1)} %get-tuple-element.4.own_input, f32[640,1280]{1,0:T(8,128)S(1)} %get-tuple-element.5.weight_grad), custom_call_target="tpu_custom_call" | custom-call | tf_op jit(solution)/shard_map/pallas_call | solution.py:628

commit v7 on v6

--- a/solution.py
+++ b/solution.py
@@ -574,8 +574,11 @@
 def put_out(own_input, weight_grad, inputs_out, weights_out, sems):
     copies = [
         pltpu.make_async_copy(own_input, inputs_out.at[0], sems.at[0]),
-        pltpu.make_async_copy(weight_grad, weights_out.at[0], sems.at[1]),
     ]
+    share = weight_grad.shape[0] // 4
+    for i in range(4):
+        part = pl.ds(i * share, share)
+        copies.append(pltpu.make_async_copy(weight_grad.at[part], weights_out.at[0, part], sems.at[1 + i]))
     for copy in copies:
         copy.start()
     for copy in copies:
@@ -633,7 +636,7 @@
         ),
         in_specs=[inside, inside],
         out_specs=(outside, outside),
-        scratch_shapes=[dma((2,))],
+        scratch_shapes=[dma((5,))],
         compiler_params=pltpu.CompilerParams(vmem_limit_bytes=6 * 1024 * 1024),
     )(own_input, weight_grad)
 

time: 154 us -> 154 us (level)
  no operation moved by 1% of the time
where the time goes in v7:
time: 154 us
  Pallas kernels  153 us (99%)
    pallas_call x1, Pallas kernels, on_device(): pl.pallas_call(relay, out_shape=(vmem((rows, width), BF16), vmem((quarter...  151 us

profile of v7, /device:TPU:40, one launch (start us, length us, event | category | flops | bytes accessed | tf_op | source)
XLA Modules:
  0.0 153.6 jit_solution(2726741964414141564)
XLA Ops:
  0.6 150.7 %shard_map.50 = (bf16[128,5120]{1,0:T(8,128)(2,1)S(1)}, f32[640,1280]{1,0:T(8,128)S(1)}) custom-call(bf16[128,5120]{1,0:T(8,128)(2,1)} %og.1, bf16[5120,1280]{1,0:T(8,128)(2,1)} %bitcast.2, bf16[128,5120]{1,0:T(8,128)(2,1)} %bitcast.3), custom_call_target="tpu_custom_call" | custom-call | tf_op jit(solution)/shard_map/pallas_call | solution.py:598
  151.3 2.2 %shard_map.51 = (bf16[1,128,5120]{2,1,0:T(8,128)(2,1)}, f32[1,640,1280]{2,1,0:T(8,128)}) custom-call(bf16[128,5120]{1,0:T(8,128)(2,1)S(1)} %get-tuple-element.4.own_input, f32[640,1280]{1,0:T(8,128)S(1)} %get-tuple-element.5.weight_grad), custom_call_target="tpu_custom_call" | custom-call | tf_op jit(solution)/shard_map/pallas_call | solution.py:631
